TPU v7x, 512 devices: a whole 4x8x8 slice. The times are simulated.
512 devices in a mesh: chain: 8 (over x, core), tile: 64 (over y, z).
Axes of the slice: x: 4, y: 8, z: 8, core: 2. Of those that a mesh axis runs over, the one named last changes fastest.
Arguments:
- right_side: float32 [3, 2, 32, 32768], P(None, None, None, ('chain', 'tile')), may hold values from -6 to 6
- diag_inverse: float32 [2, 32768, 4096], P(None, ('chain', 'tile'))
- coupling: float32 [2, 32768, 4096], P(None, ('chain', 'tile')), may hold values from -0.0390625 to 0.0390625
- updates: float32 [131072, 192], P(('chain', 'tile')), may hold values from -2.4 to 2.4
- update_rows: int32 [131072], P(('chain', 'tile')), may hold values from 0 to 4095, as said below
- tile_counts: int32 [1024], P(('chain', 'tile')), may hold values from 32 to 128, as said below
Outputs:
- solution: float32 [3, 2, 32, 32768], P(None, None, None, ('chain', 'tile'))
Inputs may be any that keep to these rules, and one draw needn't show every extreme that they name: `update_rows`: rows are counted within the supernode of the group that holds the entry. In each aligned block of 256 entries (the update rows of one device) at most 8 entries fall in any one aligned range of 64 rows, and in each run of 64 aligned blocks one such range receives exactly 8 entries from every block of the run. Padding rows carry entries too. `tile_counts`: one tile has all 128 rows live.
All inputs are finite; a program needn't handle non-finite values.
Results may differ from a plain program's by a relative error of at most 0.0001.
Values sent between devices are 32-bit elements; how exact they have to be, the bound alone decides.
A program may use at most 64 MiB of HBM per device.

v0:
```python
import jax
import jax.numpy as jnp
from jax import lax
from jax.sharding import PartitionSpec as P

highest = lax.Precision.HIGHEST


def shifted(value, axis, by):
    peers = lax.axis_size(axis)
    pairs = [(i, i + by) for i in range(peers) if 0 <= i + by < peers]
    return lax.ppermute(value, axis, pairs)


def combine_parts(products):
    return jnp.stack([products[0, 0] - products[1, 1], products[0, 1] + products[1, 0]], axis=0)


def body(right_side, diag_inverse, coupling, updates, update_rows, tile_counts):
    batches, halves, sources, own_rows = right_side.shape
    chain_size = lax.axis_size("chain")
    full_rows = diag_inverse.shape[2]
    row_count = updates.shape[0]
    tile_rows = row_count // tile_counts.shape[0]
    limits = jnp.broadcast_to(tile_counts[:, None], (tile_counts.shape[0], tile_rows)).reshape(-1)
    is_live = jnp.arange(row_count, dtype=jnp.int32) % tile_rows < limits
    live_updates = jnp.where(is_live[:, None], updates, 0.0)
    dense_sum = jax.ops.segment_sum(live_updates, update_rows, num_segments=full_rows)
    accumulated = lax.psum_scatter(dense_sum, "tile", scatter_dimension=0, tiled=True)
    arranged = accumulated.reshape(own_rows, batches, halves, sources).transpose(1, 2, 3, 0)
    reduced_all = right_side - arranged
    chain_index = lax.axis_index("chain")
    section_count = chain_size + batches - 1

    def accumulate(columns):
        diag_part = jnp.einsum("jrs,kis->kjri", columns, diag_inverse, precision=highest)
        couple_part = jnp.einsum("jrs,kis->kjri", columns, coupling, precision=highest)
        return (diag_part, couple_part)

    def advance(section_index, loop_state):
        carried, solution = loop_state
        incoming = shifted(carried, "chain", 1)
        batch_index = section_index - chain_index
        active = (batch_index >= 0) & (batch_index < batches)
        clamped = jnp.clip(batch_index, 0, batches - 1)
        reduced = lax.dynamic_index_in_dim(reduced_all, clamped, 0, keepdims=False) - incoming
        diag_sum, couple_sum = accumulate(lax.all_gather(reduced, "tile", axis=2, tiled=True))
        updated = lax.dynamic_update_index_in_dim(solution, combine_parts(diag_sum), clamped, 0)
        return (combine_parts(couple_sum), jnp.where(active, updated, solution))

    start_state = (jnp.zeros((2, sources, own_rows), jnp.float32), jnp.zeros_like(right_side))
    final_carry, solution = lax.fori_loop(0, section_count, advance, start_state)
    return solution


def solution(mesh):
    in_specs = (
        P(None, None, None, ("chain", "tile")),
        P(None, ("chain", "tile"), None),
        P(None, ("chain", "tile"), None),
        P(("chain", "tile"), None),
        P(("chain", "tile")),
        P(("chain", "tile")),
    )
    out_specs = P(None, None, None, ("chain", "tile"))
    return jax.shard_map(body, mesh=mesh, in_specs=in_specs, out_specs=out_specs, check_vma=False)
```

profile of v0, /device:TPU:2, one launch (start us, length us, event | category | flops | bytes accessed | tf_op | source)
XLA Modules:
  0.0 1293.3 jit_solution(14064460779872113943)
XLA Ops:
  8.3 4.2 scatter_custom_fusion
  12.6 251.8 %reduce-scatter.2.cloned.1.call-done = f32[64,192]{1,0:T(8,128)} async-done(((f32[4096,192]{1,0:T(8,128)}), f32[64,192]{1,0:T(8,128)}) %reduce-scatter.2.cloned.1.call-update) | async-done | bytes 49168 | tf_op jit(solution)/shard_map/reduce_scatter | solution.py:29
  265.4 1020.7 %while.15 = (s32[]{:T(128)}, f32[2,32,64]{2,1,0:T(8,128)S(1)}, f32[3,2,32,64]{3,2,1,0:T(8,128)S(1)}, s32[]{:T(128)}, f32[3,2,32,64]{3,2,1,0:T(8,128)S(1)}, /*ind...) while((s32[]{:T(128)}, f32[2,32,64]{2,1,0:T(8,128)S(1)}, ...), condition=%wide.region_3.4_spmd, body=%wide.region_2.3_spmd.sunk | while | flops 805330944 | bytes 23675160 | solution.py:52
  267.6 3.5 collective-permute-done
  271.9 84.3 %all-gather.2.cloned.1.call-done = f32[2,32,4096]{1,0,2:T(2,128)} async-done(((f32[2,32,64]{1,0,2:T(2,128)}), f32[2,32,4096]{1,0,2:T(2,128)}) %all-gather.2.cloned.1.call-update) | async-done | bytes 1048592 | tf_op jit(solution)/shard_map/while/body/eval_jaxpr/all_gather | solution.py:47
  356.2 5.2 copy.48
  361.4 3.1 fusion.38
  364.6 3.1 fusion.41
  370.0 3.5 collective-permute-done
  374.2 84.0 %all-gather.2.cloned.1.call-done = f32[2,32,4096]{1,0,2:T(2,128)} async-done(((f32[2,32,64]{1,0,2:T(2,128)}), f32[2,32,4096]{1,0,2:T(2,128)}) %all-gather.2.cloned.1.call-update) | async-done | bytes 1048592 | tf_op jit(solution)/shard_map/while/body/eval_jaxpr/all_gather | solution.py:47
  458.2 5.2 copy.48
  466.6 3.1 fusion.41
  472.0 3.5 collective-permute-done
  476.3 84.0 %all-gather.2.cloned.1.call-done = f32[2,32,4096]{1,0,2:T(2,128)} async-done(((f32[2,32,64]{1,0,2:T(2,128)}), f32[2,32,4096]{1,0,2:T(2,128)}) %all-gather.2.cloned.1.call-update) | async-done | bytes 1048592 | tf_op jit(solution)/shard_map/while/body/eval_jaxpr/all_gather | solution.py:47
  560.3 5.2 copy.48
  565.5 3.1 fusion.38
  568.7 3.1 fusion.41
  574.1 3.5 collective-permute-done
  578.3 84.0 %all-gather.2.cloned.1.call-done = f32[2,32,4096]{1,0,2:T(2,128)} async-done(((f32[2,32,64]{1,0,2:T(2,128)}), f32[2,32,4096]{1,0,2:T(2,128)}) %all-gather.2.cloned.1.call-update) | async-done | bytes 1048592 | tf_op jit(solution)/shard_map/while/body/eval_jaxpr/all_gather | solution.py:47
  662.3 5.2 copy.48
  667.6 3.1 fusion.38
  670.7 3.1 fusion.41
  676.1 3.5 collective-permute-done
  680.4 84.0 %all-gather.2.cloned.1.call-done = f32[2,32,4096]{1,0,2:T(2,128)} async-done(((f32[2,32,64]{1,0,2:T(2,128)}), f32[2,32,4096]{1,0,2:T(2,128)}) %all-gather.2.cloned.1.call-update) | async-done | bytes 1048592 | tf_op jit(solution)/shard_map/while/body/eval_jaxpr/all_gather | solution.py:47
  764.4 5.2 copy.48
  772.8 3.1 fusion.41
  778.2 3.5 collective-permute-done
  782.4 84.0 %all-gather.2.cloned.1.call-done = f32[2,32,4096]{1,0,2:T(2,128)} async-done(((f32[2,32,64]{1,0,2:T(2,128)}), f32[2,32,4096]{1,0,2:T(2,128)}) %all-gather.2.cloned.1.call-update) | async-done | bytes 1048592 | tf_op jit(solution)/shard_map/while/body/eval_jaxpr/all_gather | solution.py:47
  866.4 5.2 copy.48
  874.8 3.1 fusion.41
  880.2 3.5 collective-permute-done
  884.4 84.0 %all-gather.2.cloned.1.call-done = f32[2,32,4096]{1,0,2:T(2,128)} async-done(((f32[2,32,64]{1,0,2:T(2,128)}), f32[2,32,4096]{1,0,2:T(2,128)}) %all-gather.2.cloned.1.call-update) | async-done | bytes 1048592 | tf_op jit(solution)/shard_map/while/body/eval_jaxpr/all_gather | solution.py:47
  968.4 5.2 copy.48
  973.7 3.1 fusion.38
  976.8 3.1 fusion.41
  982.2 3.5 collective-permute-done
  986.5 84.0 %all-gather.2.cloned.1.call-done = f32[2,32,4096]{1,0,2:T(2,128)} async-done(((f32[2,32,64]{1,0,2:T(2,128)}), f32[2,32,4096]{1,0,2:T(2,128)}) %all-gather.2.cloned.1.call-update) | async-done | bytes 1048592 | tf_op jit(solution)/shard_map/while/body/eval_jaxpr/all_gather | solution.py:47
  1070.5 5.2 copy.48
  1075.7 3.1 fusion.38
  1078.9 3.1 fusion.41
  1084.3 3.5 collective-permute-done
  1088.5 84.0 %all-gather.2.cloned.1.call-done = f32[2,32,4096]{1,0,2:T(2,128)} async-done(((f32[2,32,64]{1,0,2:T(2,128)}), f32[2,32,4096]{1,0,2:T(2,128)}) %all-gather.2.cloned.1.call-update) | async-done | bytes 1048592 | tf_op jit(solution)/shard_map/while/body/eval_jaxpr/all_gather | solution.py:47
  1172.5 5.2 copy.48
  1180.9 3.1 fusion.41
  1186.3 3.5 collective-permute-done
  1190.5 84.0 %all-gather.2.cloned.1.call-done = f32[2,32,4096]{1,0,2:T(2,128)} async-done(((f32[2,32,64]{1,0,2:T(2,128)}), f32[2,32,4096]{1,0,2:T(2,128)}) %all-gather.2.cloned.1.call-update) | async-done | bytes 1048592 | tf_op jit(solution)/shard_map/while/body/eval_jaxpr/all_gather | solution.py:47
  1274.5 5.2 copy.48
  1283.0 3.1 fusion.41
  (170 shorter events, 47.9 us)
Async XLA Ops:
  6.5 257.9 %reduce-scatter.2.cloned.1.call-start = ((), (), s32[]{:S(2)}) async-start(), calls=%async_computation.1 | async-start | bytes 4259840 | tf_op jit(solution)/shard_map/reduce_scatter | solution.py:29
  12.6 252.8 %copy-start.3 = (f32[3,2,32,64]{3,2,1,0:T(8,128)S(1)}, f32[3,2,32,64]{3,2,1,0:T(8,128)}, u32[]{:S(2)}) copy-start(f32[3,2,32,64]{3,2,1,0:T(8,128)} %param.8) | copy-start | bytes 147460
  12.6 252.8 %copy-start = (f32[2,64,4096]{2,1,0:T(8,128)S(1)}, f32[2,64,4096]{2,1,0:T(8,128)}, u32[]{:S(2)}) copy-start(f32[2,64,4096]{2,1,0:T(8,128)} %param.10) | copy-start | bytes 6291460
  265.4 90.8 %all-gather.2.cloned.1.call-start = ((), (), s32[]{:S(2)}) async-start(), calls=%async_computation.2 | async-start | bytes 4259840 | tf_op jit(solution)/shard_map/while/body/eval_jaxpr/all_gather | solution.py:47
  265.6 5.6 collective-permute-start
  361.4 3.2 copy-start.1
  367.8 90.4 %all-gather.2.cloned.1.call-start = ((), (), s32[]{:S(2)}) async-start(), calls=%async_computation.2 | async-start | bytes 4259840 | tf_op jit(solution)/shard_map/while/body/eval_jaxpr/all_gather | solution.py:47
  368.0 5.6 collective-permute-start
  463.5 3.2 copy-start.1
  469.9 90.4 %all-gather.2.cloned.1.call-start = ((), (), s32[]{:S(2)}) async-start(), calls=%async_computation.2 | async-start | bytes 4259840 | tf_op jit(solution)/shard_map/while/body/eval_jaxpr/all_gather | solution.py:47
  470.0 5.6 collective-permute-start
  565.5 3.2 copy-start.1
  571.9 90.4 %all-gather.2.cloned.1.call-start = ((), (), s32[]{:S(2)}) async-start(), calls=%async_computation.2 | async-start | bytes 4259840 | tf_op jit(solution)/shard_map/while/body/eval_jaxpr/all_gather | solution.py:47
  572.0 5.6 collective-permute-start
  667.6 3.2 copy-start.1
  673.9 90.4 %all-gather.2.cloned.1.call-start = ((), (), s32[]{:S(2)}) async-start(), calls=%async_computation.2 | async-start | bytes 4259840 | tf_op jit(solution)/shard_map/while/body/eval_jaxpr/all_gather | solution.py:47
  674.1 5.6 collective-permute-start
  769.6 3.2 copy-start.1
  776.0 90.4 %all-gather.2.cloned.1.call-start = ((), (), s32[]{:S(2)}) async-start(), calls=%async_computation.2 | async-start | bytes 4259840 | tf_op jit(solution)/shard_map/while/body/eval_jaxpr/all_gather | solution.py:47
  776.1 5.6 collective-permute-start
  871.6 3.2 copy-start.1
  878.0 90.4 %all-gather.2.cloned.1.call-start = ((), (), s32[]{:S(2)}) async-start(), calls=%async_computation.2 | async-start | bytes 4259840 | tf_op jit(solution)/shard_map/while/body/eval_jaxpr/all_gather | solution.py:47
  878.2 5.6 collective-permute-start
  973.7 3.2 copy-start.1
  980.0 90.4 %all-gather.2.cloned.1.call-start = ((), (), s32[]{:S(2)}) async-start(), calls=%async_computation.2 | async-start | bytes 4259840 | tf_op jit(solution)/shard_map/while/body/eval_jaxpr/all_gather | solution.py:47
  980.2 5.6 collective-permute-start
  1075.7 3.2 copy-start.1
  1082.1 90.4 %all-gather.2.cloned.1.call-start = ((), (), s32[]{:S(2)}) async-start(), calls=%async_computation.2 | async-start | bytes 4259840 | tf_op jit(solution)/shard_map/while/body/eval_jaxpr/all_gather | solution.py:47
  1082.2 5.6 collective-permute-start
  1177.7 3.2 copy-start.1
  1184.1 90.4 %all-gather.2.cloned.1.call-start = ((), (), s32[]{:S(2)}) async-start(), calls=%async_computation.2 | async-start | bytes 4259840 | tf_op jit(solution)/shard_map/while/body/eval_jaxpr/all_gather | solution.py:47
  1184.3 5.6 collective-permute-start
  1279.8 3.2 copy-start.1
  1286.2 0.6 copy-start.2
Sparse Core Ops, SparseCore 0:
  12.7 251.6 reduce-scatter.1
  272.0 84.1 all-gather.1
  374.4 83.8 all-gather.1
  476.4 83.8 all-gather.1
  578.4 83.8 all-gather.1
  680.5 83.8 all-gather.1
  782.5 83.8 all-gather.1
  884.5 83.8 all-gather.1
  986.6 83.8 all-gather.1
  1088.6 83.8 all-gather.1
  1190.7 83.8 all-gather.1
where the time goes:
time: 1290 us
  waiting for transfers between devices  1130 us (88%)
  matrix products  62.5 us (5%)
  local copies, waits for them, and re-layouts  56.1 us (4%)
  starting transfers between devices  19.6 us (2%)
  between operations  13.1 us (1%)
  other arithmetic  13 us (1%)
    all_gather x10, waiting for transfers between devices, advance(): lax.all_gather(reduced, 'tile', axis=2, tiled=True)  840 us
    reduce_scatter x1, waiting for transfers between devices, body(): lax.psum_scatter(dense_sum, 'tile', scatter_dimension=0, tiled=True)  252 us
    all_gather x10, local copies, waits for them, and re-layouts, advance(): lax.all_gather(reduced, 'tile', axis=2, tiled=True)  52.3 us
    ppermute x10, waiting for transfers between devices, shifted(): return lax.ppermute(value, axis, pairs)  35.4 us
    dot_general x10, matrix products, accumulate(): jnp.einsum('jrs,kis->kjri', columns, diag_inverse, precision=highest)  31.3 us
    dot_general x10, matrix products, accumulate(): jnp.einsum('jrs,kis->kjri', columns, coupling, precision=highest)  31.2 us
  transfers between devices with their start and end apart: 21, of which 21 were waited for; matrix products, arithmetic and copies ran while one was open for 0% of the time, Pallas kernels for 0%

commit v1 on v0

--- a/solution.py
+++ b/solution.py
@@ -4,6 +4,11 @@
 from jax.sharding import PartitionSpec as P
 
 highest = lax.Precision.HIGHEST
+
+
+def tiled_gather(x, axis, dim):
+    copies = jnp.concatenate([x] * lax.axis_size(axis), axis=dim)
+    return lax.all_to_all(copies, axis, dim, dim, tiled=True)
 
 
 def shifted(value, axis, by):
@@ -44,7 +49,7 @@
         active = (batch_index >= 0) & (batch_index < batches)
         clamped = jnp.clip(batch_index, 0, batches - 1)
         reduced = lax.dynamic_index_in_dim(reduced_all, clamped, 0, keepdims=False) - incoming
-        diag_sum, couple_sum = accumulate(lax.all_gather(reduced, "tile", axis=2, tiled=True))
+        diag_sum, couple_sum = accumulate(tiled_gather(reduced, "tile", 2))
         updated = lax.dynamic_update_index_in_dim(solution, combine_parts(diag_sum), clamped, 0)
         return (combine_parts(couple_sum), jnp.where(active, updated, solution))
 

time: 1290 us -> 1060 us (0.82)
  the two profiles are of different devices: /device:TPU:2 before, /device:TPU:16 now
where the time goes in v1:
time: 1060 us
  waiting for transfers between devices  559 us (53%)
  local copies, waits for them, and re-layouts  273 us (26%)
  starting transfers between devices  92.3 us (9%)
  matrix products  78.4 us (7%)
  other arithmetic  38.9 us (4%)
  between operations  13.5 us (1%)
    all_to_all x10, waiting for transfers between devices, tiled_gather(): return lax.all_to_all(copies, axis, dim, dim, tiled=True)  299 us
    reduce_scatter x1, waiting for transfers between devices, body(): lax.psum_scatter(dense_sum, 'tile', scatter_dimension=0, tiled=True)  252 us
    while x40, local copies, waits for them, and re-layouts  114 us
    all_to_all x30, local copies, waits for them, and re-layouts, tiled_gather(): return lax.all_to_all(copies, axis, dim, dim, tiled=True)  106 us
    all_to_all x10, starting transfers between devices, tiled_gather(): return lax.all_to_all(copies, axis, dim, dim, tiled=True)  63.9 us
    concatenate x20, local copies, waits for them, and re-layouts, tiled_gather(): copies = jnp.concatenate([x] * lax.axis_size(axis), axis=dim)  50.9 us
    dot_general x10, matrix products, accumulate(): jnp.einsum('jrs,kis->kjri', columns, diag_inverse, precision=highest)  47.2 us
    all_to_all x10, other arithmetic, tiled_gather(): return lax.all_to_all(copies, axis, dim, dim, tiled=True)  32.5 us
  transfers between devices with their start and end apart: 21, of which 21 were waited for; matrix products, arithmetic and copies ran while one was open for 0% of the time, Pallas kernels for 0%

profile of v1, /device:TPU:16, one launch (start us, length us, event | category | flops | bytes accessed | tf_op | source)
XLA Modules:
  0.0 1056.4 jit_solution(2679140568349875855)
XLA Ops:
  12.6 251.6 %reduce-scatter.2.cloned.1.call-done = f32[64,192]{1,0:T(8,128)} async-done(((f32[4096,192]{1,0:T(8,128)}), f32[64,192]{1,0:T(8,128)}) %reduce-scatter.2.cloned.1.call-update) | async-done | bytes 49168 | tf_op jit(solution)/shard_map/reduce_scatter | solution.py:34
  265.2 783.8 %while.15 = (s32[]{:T(128)}, f32[2,32,64]{2,1,0:T(8,128)S(1)}, f32[3,2,32,64]{3,2,1,0:T(8,128)S(1)}, s32[]{:T(128)}, f32[3,2,32,64]{3,2,1,0:T(8,128)S(1)}, /*ind...) while((s32[]{:T(128)}, f32[2,32,64]{2,1,0:T(8,128)S(1)}, ...), condition=%wide.region_3.4_spmd, body=%wide.region_2.3_spmd.sunk | while | flops 805330944 | bytes 32915748 | solution.py:57
  272.6 6.5 reshape.130
  279.1 9.2 all-to-all-start
  288.4 28.9 %all-to-all-done = f32[64,1,4096]{2,1,0:T(1,128)S(1)} async-done(((f32[64,1,4096]{2,1,0:T(1,128)}), f32[64,1,4096]{2,1,0:T(1,128)S(1)}, u32[]{:S(2)}, u32[]{:S(2)}) %all-to-all-start) | async-done | bytes 1048608 | tf_op jit(solution)/shard_map/while/body/eval_jaxpr/all_to_all | solution.py:11
  321.1 4.9 reshape.131
  330.6 5.4 copy.55
  354.5 6.5 reshape.130
  361.0 6.1 all-to-all-start
  367.1 28.8 %all-to-all-done = f32[64,1,4096]{2,1,0:T(1,128)S(1)} async-done(((f32[64,1,4096]{2,1,0:T(1,128)}), f32[64,1,4096]{2,1,0:T(1,128)S(1)}, u32[]{:S(2)}, u32[]{:S(2)}) %all-to-all-start) | async-done | bytes 1048608 | tf_op jit(solution)/shard_map/while/body/eval_jaxpr/all_to_all | solution.py:11
  409.3 5.4 copy.55
  422.6 4.9 collective-permute-start
  433.4 6.5 reshape.130
  439.9 5.5 all-to-all-start
  445.5 28.2 %all-to-all-done = f32[64,1,4096]{2,1,0:T(1,128)S(1)} async-done(((f32[64,1,4096]{2,1,0:T(1,128)}), f32[64,1,4096]{2,1,0:T(1,128)S(1)}, u32[]{:S(2)}, u32[]{:S(2)}) %all-to-all-start) | async-done | bytes 1048608 | tf_op jit(solution)/shard_map/while/body/eval_jaxpr/all_to_all | solution.py:11
  487.0 5.4 copy.55
  500.3 5.4 collective-permute-start
  511.6 6.5 reshape.130
  518.1 5.7 all-to-all-start
  523.9 28.9 %all-to-all-done = f32[64,1,4096]{2,1,0:T(1,128)S(1)} async-done(((f32[64,1,4096]{2,1,0:T(1,128)}), f32[64,1,4096]{2,1,0:T(1,128)S(1)}, u32[]{:S(2)}, u32[]{:S(2)}) %all-to-all-start) | async-done | bytes 1048608 | tf_op jit(solution)/shard_map/while/body/eval_jaxpr/all_to_all | solution.py:11
  556.5 4.9 reshape.131
  566.1 5.4 copy.55
  590.0 6.5 reshape.130
  596.5 5.9 all-to-all-start
  602.4 30.6 %all-to-all-done = f32[64,1,4096]{2,1,0:T(1,128)S(1)} async-done(((f32[64,1,4096]{2,1,0:T(1,128)}), f32[64,1,4096]{2,1,0:T(1,128)S(1)}, u32[]{:S(2)}, u32[]{:S(2)}) %all-to-all-start) | async-done | bytes 1048608 | tf_op jit(solution)/shard_map/while/body/eval_jaxpr/all_to_all | solution.py:11
  646.3 5.4 copy.55
  668.2 6.5 reshape.130
  674.7 6.4 all-to-all-start
  681.1 30.7 %all-to-all-done = f32[64,1,4096]{2,1,0:T(1,128)S(1)} async-done(((f32[64,1,4096]{2,1,0:T(1,128)}), f32[64,1,4096]{2,1,0:T(1,128)S(1)}, u32[]{:S(2)}, u32[]{:S(2)}) %all-to-all-start) | async-done | bytes 1048608 | tf_op jit(solution)/shard_map/while/body/eval_jaxpr/all_to_all | solution.py:11
  725.2 5.4 copy.55
  745.8 6.5 reshape.130
  752.3 6.2 all-to-all-start
  758.5 30.9 %all-to-all-done = f32[64,1,4096]{2,1,0:T(1,128)S(1)} async-done(((f32[64,1,4096]{2,1,0:T(1,128)}), f32[64,1,4096]{2,1,0:T(1,128)S(1)}, u32[]{:S(2)}, u32[]{:S(2)}) %all-to-all-start) | async-done | bytes 1048608 | tf_op jit(solution)/shard_map/while/body/eval_jaxpr/all_to_all | solution.py:11
  802.8 5.4 copy.55
  823.3 6.5 reshape.130
  829.8 6.3 all-to-all-start
  836.2 30.9 %all-to-all-done = f32[64,1,4096]{2,1,0:T(1,128)S(1)} async-done(((f32[64,1,4096]{2,1,0:T(1,128)}), f32[64,1,4096]{2,1,0:T(1,128)S(1)}, u32[]{:S(2)}, u32[]{:S(2)}) %all-to-all-start) | async-done | bytes 1048608 | tf_op jit(solution)/shard_map/while/body/eval_jaxpr/all_to_all | solution.py:11
  870.8 4.9 reshape.131
  880.4 5.4 copy.55
  901.0 6.5 reshape.130
  907.5 6.3 all-to-all-start
  913.8 30.9 %all-to-all-done = f32[64,1,4096]{2,1,0:T(1,128)S(1)} async-done(((f32[64,1,4096]{2,1,0:T(1,128)}), f32[64,1,4096]{2,1,0:T(1,128)S(1)}, u32[]{:S(2)}, u32[]{:S(2)}) %all-to-all-start) | async-done | bytes 1048608 | tf_op jit(solution)/shard_map/while/body/eval_jaxpr/all_to_all | solution.py:11
  958.0 5.4 copy.55
  978.6 6.5 reshape.130
  985.1 6.3 all-to-all-start
  991.4 30.9 %all-to-all-done = f32[64,1,4096]{2,1,0:T(1,128)S(1)} async-done(((f32[64,1,4096]{2,1,0:T(1,128)}), f32[64,1,4096]{2,1,0:T(1,128)S(1)}, u32[]{:S(2)}, u32[]{:S(2)}) %all-to-all-start) | async-done | bytes 1048608 | tf_op jit(solution)/shard_map/while/body/eval_jaxpr/all_to_all | solution.py:11
  1026.0 4.9 reshape.131
  1035.6 5.4 copy.55
  (198 shorter events, 278.1 us)
Async XLA Ops:
  6.5 257.6 %reduce-scatter.2.cloned.1.call-start = ((), (), s32[]{:S(2)}) async-start(), calls=%async_computation.2 | async-start | bytes 4259840 | tf_op jit(solution)/shard_map/reduce_scatter | solution.py:34
  8.3 256.8 %copy-start.2 = (f32[3,2,32,64]{3,2,1,0:T(8,128)S(1)}, f32[3,2,32,64]{3,2,1,0:T(8,128)}, u32[]{:S(2)}) copy-start(f32[3,2,32,64]{3,2,1,0:T(8,128)} %param.8) | copy-start | bytes 147460
  265.4 2.1 collective-permute-start
  279.1 38.2 %all-to-all-start = ((f32[64,1,4096]{2,1,0:T(1,128)}), f32[64,1,4096]{2,1,0:T(1,128)S(1)}, u32[]{:S(2)}, u32[]{:S(2)}) async-start(f32[64,1,4096]{2,1,0:T(1,128)} %reshape.130), calls=%async_computation | async-start | bytes 2097152 | tf_op jit(solution)/shard_map/while/body/eval_jaxpr/all_to_all | solution.py:11
  330.6 10.1 copy-start
  344.0 5.5 collective-permute-start
  361.0 34.8 %all-to-all-start = ((f32[64,1,4096]{2,1,0:T(1,128)}), f32[64,1,4096]{2,1,0:T(1,128)S(1)}, u32[]{:S(2)}, u32[]{:S(2)}) async-start(f32[64,1,4096]{2,1,0:T(1,128)} %reshape.130), calls=%async_computation | async-start | bytes 2097152 | tf_op jit(solution)/shard_map/while/body/eval_jaxpr/all_to_all | solution.py:11
  409.3 10.1 copy-start
  422.6 5.7 collective-permute-start
  439.9 33.7 %all-to-all-start = ((f32[64,1,4096]{2,1,0:T(1,128)}), f32[64,1,4096]{2,1,0:T(1,128)S(1)}, u32[]{:S(2)}, u32[]{:S(2)}) async-start(f32[64,1,4096]{2,1,0:T(1,128)} %reshape.130), calls=%async_computation | async-start | bytes 2097152 | tf_op jit(solution)/shard_map/while/body/eval_jaxpr/all_to_all | solution.py:11
  487.0 10.1 copy-start
  500.3 6.2 collective-permute-start
  518.1 34.6 %all-to-all-start = ((f32[64,1,4096]{2,1,0:T(1,128)}), f32[64,1,4096]{2,1,0:T(1,128)S(1)}, u32[]{:S(2)}, u32[]{:S(2)}) async-start(f32[64,1,4096]{2,1,0:T(1,128)} %reshape.130), calls=%async_computation | async-start | bytes 2097152 | tf_op jit(solution)/shard_map/while/body/eval_jaxpr/all_to_all | solution.py:11
  566.1 10.1 copy-start
  579.5 5.4 collective-permute-start
  596.5 36.5 %all-to-all-start = ((f32[64,1,4096]{2,1,0:T(1,128)}), f32[64,1,4096]{2,1,0:T(1,128)S(1)}, u32[]{:S(2)}, u32[]{:S(2)}) async-start(f32[64,1,4096]{2,1,0:T(1,128)} %reshape.130), calls=%async_computation | async-start | bytes 2097152 | tf_op jit(solution)/shard_map/while/body/eval_jaxpr/all_to_all | solution.py:11
  646.3 10.1 copy-start
  659.7 3.5 collective-permute-start
  674.7 37.1 %all-to-all-start = ((f32[64,1,4096]{2,1,0:T(1,128)}), f32[64,1,4096]{2,1,0:T(1,128)S(1)}, u32[]{:S(2)}, u32[]{:S(2)}) async-start(f32[64,1,4096]{2,1,0:T(1,128)} %reshape.130), calls=%async_computation | async-start | bytes 2097152 | tf_op jit(solution)/shard_map/while/body/eval_jaxpr/all_to_all | solution.py:11
  725.2 10.1 copy-start
  738.5 2.1 collective-permute-start
  752.3 37.1 %all-to-all-start = ((f32[64,1,4096]{2,1,0:T(1,128)}), f32[64,1,4096]{2,1,0:T(1,128)S(1)}, u32[]{:S(2)}, u32[]{:S(2)}) async-start(f32[64,1,4096]{2,1,0:T(1,128)} %reshape.130), calls=%async_computation | async-start | bytes 2097152 | tf_op jit(solution)/shard_map/while/body/eval_jaxpr/all_to_all | solution.py:11
  802.8 10.1 copy-start
  816.1 2.1 collective-permute-start
  829.8 37.2 %all-to-all-start = ((f32[64,1,4096]{2,1,0:T(1,128)}), f32[64,1,4096]{2,1,0:T(1,128)S(1)}, u32[]{:S(2)}, u32[]{:S(2)}) async-start(f32[64,1,4096]{2,1,0:T(1,128)} %reshape.130), calls=%async_computation | async-start | bytes 2097152 | tf_op jit(solution)/shard_map/while/body/eval_jaxpr/all_to_all | solution.py:11
  880.4 10.1 copy-start
  893.7 2.1 collective-permute-start
  907.5 37.2 %all-to-all-start = ((f32[64,1,4096]{2,1,0:T(1,128)}), f32[64,1,4096]{2,1,0:T(1,128)S(1)}, u32[]{:S(2)}, u32[]{:S(2)}) async-start(f32[64,1,4096]{2,1,0:T(1,128)} %reshape.130), calls=%async_computation | async-start | bytes 2097152 | tf_op jit(solution)/shard_map/while/body/eval_jaxpr/all_to_all | solution.py:11
  958.0 10.1 copy-start
  971.3 2.1 collective-permute-start
  985.1 37.2 %all-to-all-start = ((f32[64,1,4096]{2,1,0:T(1,128)}), f32[64,1,4096]{2,1,0:T(1,128)S(1)}, u32[]{:S(2)}, u32[]{:S(2)}) async-start(f32[64,1,4096]{2,1,0:T(1,128)} %reshape.130), calls=%async_computation | async-start | bytes 2097152 | tf_op jit(solution)/shard_map/while/body/eval_jaxpr/all_to_all | solution.py:11
  1035.6 10.1 copy-start
  1049.0 0.6 copy-start.1
Sparse Core Ops, SparseCore 0:
  12.7 251.3 reduce-scatter.1
